TPU v7x, 32 devices: a whole 2x2x4 slice. The times are simulated.
32 devices in a mesh: tok: 8 (over z, y), exp: 4 (over x, core).
Axes of the slice: x: 2, y: 2, z: 4, core: 2. Of those that a mesh axis runs over, the one named last changes fastest.
Arguments:
- tokens: bfloat16 [12, 8192, 1024], P(None, 'tok'), may hold values from -24 to 24
- slot_params: bfloat16 [1024, 128], P(None, 'exp'), may hold values from -2 to 2
- w_in: bfloat16 [64, 1024, 4096], P('exp', None, 'tok'), may hold values from -0.75 to 0.75
- w_out: bfloat16 [64, 4096, 1024], P('exp', 'tok'), may hold values from -0.1875 to 0.1875
Outputs:
- mixed: bfloat16 [12, 8192, 1024], P(None, 'tok', 'exp')
All inputs are finite; a program needn't handle non-finite values.
Results may differ from a plain program's by a relative error of at most 0.0072.
Values may be sent and summed in bfloat16 or wider, within the bound.
A program may use at most 192 MiB of HBM per device.

v0:
```python
import jax
import jax.numpy as jnp
from jax import lax
from jax.sharding import PartitionSpec as P

SLOTS_PER = 2


def shards(tokens, slot_params, w_in, w_out):
    own_width = slot_params.shape[1]
    own_logits = jnp.einsum("std,dj->sjt", tokens, slot_params, preferred_element_type=jnp.float32)
    all_logits = lax.all_gather(own_logits, "exp", axis=1, tiled=True)
    local_max = jnp.max(own_logits, axis=2)
    slot_peak = lax.pmax(local_max, "tok")
    dexp = jnp.exp(own_logits - slot_peak[:, :, None])
    local_den = jnp.sum(dexp, axis=2)
    dweight = dexp.astype(jnp.bfloat16)
    local_sum = jnp.einsum("sjt,std->sjd", dweight, tokens, preferred_element_type=jnp.float32)
    slot_sum, slot_den = lax.psum((local_sum, local_den), "tok")
    slot_in = (slot_sum / slot_den[:, :, None]).astype(jnp.bfloat16)
    seq_count = tokens.shape[0]
    local_experts = w_in.shape[0]
    width = tokens.shape[2]
    grouped = slot_in.reshape(seq_count, local_experts, SLOTS_PER, width)
    hidden = jax.nn.gelu(
        jnp.einsum("sepd,edf->sepf", grouped, w_in, preferred_element_type=jnp.float32),
        approximate=True,
    ).astype(jnp.bfloat16)
    partial_out = jnp.einsum("sepf,efd->sepd", hidden, w_out, preferred_element_type=jnp.float32)
    partial_out = partial_out.reshape(seq_count, own_width, width)
    summed = lax.psum(partial_out, "tok").astype(jnp.bfloat16)
    slot_out = lax.all_to_all(summed, "exp", split_axis=2, concat_axis=1, tiled=True)
    comb_max = jnp.max(all_logits, axis=1)
    cexp = jnp.exp(all_logits - comb_max[:, None, :])
    cweight = (cexp / jnp.sum(cexp, axis=1)[:, None, :]).astype(jnp.bfloat16)
    mixed = jnp.einsum("sjt,sjd->std", cweight, slot_out, preferred_element_type=jnp.float32)
    return mixed.astype(jnp.bfloat16)


def solution(mesh):
    return jax.shard_map(
        shards,
        mesh=mesh,
        in_specs=(
            P(None, "tok", None),
            P(None, "exp"),
            P("exp", None, "tok"),
            P("exp", "tok", None),
        ),
        out_specs=P(None, "tok", "exp"),
        check_vma=False,
    )
```

profile of v0, /device:TPU:0, one launch (start us, length us, event | category | flops | bytes accessed | tf_op | source)
XLA Modules:
  0.0 546.4 jit_solution(2624365932778062341)
XLA Ops:
  7.4 0.0 copy-start
  7.4 0.0 all-reduce.3.cloned.1.call-start
  7.4 0.8 copy-done
  8.2 12.3 %fusion.28 = (f32[12,32]{1,0:T(8,128)S(1)}, f32[12,32,1024]{2,1,0:T(8,128)S(1)}) fusion(bf16[12,1024,1024]{2,1,0:T(8,128)(2,1)} %param.4, bf16[1024,32]{0,1:T(8,128)(2,1)S(1)} %copy-done), kind=kOutput, calls=%fused_computation.28 | convolution fusion | flops 805699200 | bytes 26805760 | tf_op jit(solution)/shard_map/std,dj->sjt/dot_general | solution.py:11
  20.5 0.0 copy-start.2
  20.5 23.4 %pmax.7 = f32[12,32]{1,0:T(8,128)S(1)} all-reduce(f32[12,32]{1,0:T(8,128)S(1)} %get-tuple-element.5), channel_id=1, replica_groups=mesh['tok'=8,'exp'=4] {'tok'}, use_global_device_ids=true, to_apply=%region_3.0 | all-reduce | flops 384 | bytes 3072 | tf_op jit(solution)/shard_map/pmax | solution.py:14
  43.9 11.7 %fusion.23 = f32[12,32,1024]{2,1,0:T(8,128)} fusion(bf16[12,1024,1024]{2,1,0:T(8,128)(2,1)} %param.4, f32[12,32,1024]{2,1,0:T(8,128)S(1)} %get-tuple-element.6, f32[12,32]{1,0:T(8,128)S(1)} %pmax.7), kind=kOutput, calls=%fused_computation.24 | convolution fusion | flops 806092800 | bytes 28313088 | tf_op jit(solution)/shard_map/sjt,std->sjd/dot_general | solution.py:18
  55.6 0.0 copy-done.2
  55.6 0.0 all-reduce.3.cloned.1.call-update
  55.6 0.0 all-gather.2.cloned.1.call-start
  55.6 0.5 all-gather.2.cloned.1.call-update
  56.2 1.8 fusion.6
  57.9 18.4 %psum.22 = f32[12,32]{1,0:T(8,128)S(1)} all-reduce(f32[12,32]{1,0:T(8,128)S(1)} %fusion.6), channel_id=1, replica_groups=mesh['tok'=8,'exp'=4] {'tok'}, use_global_device_ids=true, to_apply=%region_6.0 | all-reduce | flops 384 | bytes 3072 | tf_op jit(solution)/shard_map/psum | solution.py:19
  76.3 66.0 %all-reduce.3.cloned.1.call-done = f32[12,32,1024]{2,1,0:T(8,128)} async-done(((f32[12,32,1024]{2,1,0:T(8,128)}), f32[12,32,1024]{2,1,0:T(8,128)}) %all-reduce.3.cloned.1.call-update) | async-done | bytes 1572880 | tf_op jit(solution)/shard_map/psum | solution.py:19
  142.3 1.6 divide_convert_fusion.2
  144.0 0.4 copy.20
  144.4 8.7 %fusion.20 = bf16[12,16,2,512]{3,0,2,1:T(8,128)(2,1)S(1)} fusion(bf16[12,16,2,1024]{3,0,2,1:T(8,128)(2,1)S(1)} %bitcast.48, bf16[16,1024,512]{2,1,0:T(8,128)(2,1)} %param.6), kind=kOutput, calls=%fused_computation.23 | convolution fusion | flops 404422656 | bytes 17956864 | tf_op jit(solution)/shard_map/sepd,edf->sepf/dot_general | solution.py:26
  153.2 8.7 %fusion.1 = f32[16,12,2,1024]{3,1,2,0:T(8,128)S(1)} fusion(bf16[12,16,2,512]{3,0,2,1:T(8,128)(2,1)S(1)} %fusion.20, bf16[16,512,1024]{2,1,0:T(8,128)(2,1)} %param.7), kind=kOutput, calls=%fused_computation.1 | convolution fusion | flops 402653184 | bytes 18743296 | tf_op jit(solution)/shard_map/sepf,efd->sepd/dot_general | solution.py:29
  161.9 6.5 %copy.13 = f32[12,32,1024]{1,0,2:T(8,128)} copy(f32[12,32,1024]{2,0,1:T(8,128)S(1)} %bitcast.47) | data formatting | bytes 3145728 | tf_op jit(solution)/shard_map/reshape | solution.py:30
  168.4 326.7 %all-reduce.4 = bf16[12,32,1024]{1,0,2:T(8,128)(2,1)} all-reduce(f32[12,32,1024]{1,0,2:T(8,128)} %copy.13), channel_id=1, replica_groups=mesh['tok'=8,'exp'=4] {'tok'}, use_global_device_ids=true, to_apply=%region_7.0 | all-reduce | flops 393216 | bytes 2359296 | tf_op jit(solution)/shard_map/psum | solution.py:31
  495.1 5.0 reshape.15
  500.1 14.2 %all_to_all.18 = bf16[4,2,49152]{2,1,0:T(2,128)(2,1)S(1)} all-to-all(bf16[4,2,49152]{2,1,0:T(2,128)(2,1)S(1)} %reshape.15), channel_id=1, replica_groups=mesh['tok'=8,'exp'=4] {'exp'}, dimensions={0} | all-to-all | bytes 1572864 | tf_op jit(solution)/shard_map/all_to_all | solution.py:32
  514.3 4.1 reshape.16
  518.4 5.1 copy.21
  523.6 0.1 copy.15
  523.7 0.0 all-gather.2.cloned.1.call-done
  523.7 5.8 %fusion.29 = f32[12,1024]{1,0:T(8,128)S(1)} fusion(f32[12,128,1024]{2,1,0:T(8,128)} %all-gather.2.cloned.1.call-done), kind=kOutput, calls=%fused_computation.29 | output fusion | flops 3145855 | bytes 6340608 | tf_op jit(solution)/shard_map/sub | solution.py:34
  529.5 0.0 copy-start.1
  529.6 9.4 %convolution_convert_fusion = bf16[12,1024,256]{2,1,0:T(8,128)(2,1)} fusion(bf16[12,128,256]{2,1,0:T(8,128)(2,1)S(1)} %bitcast.50, f32[12,1024]{1,0:T(8,128)S(1)} %fusion.29, f32[12,128,1024]{2,1,0:T(8,128)} %all-gather.2.cloned.1.call-done), kind=kOutput, calls=%fused_computation.7 | convolution fusion | flops 813183104 | bytes 13418496 | tf_op jit(solution)/shard_map/sjt,sjd->std/dot_general | solution.py:36
  539.0 0.0 copy-done.1
Async XLA Ops:
  7.4 0.8 copy-start
  7.4 135.0 %all-reduce.3.cloned.1.call-start = ((), (), s32[]{:S(2)}) async-start(), calls=%async_computation.2 | async-start | bytes 3145728 | tf_op jit(solution)/shard_map/psum | solution.py:19
  20.5 35.0 %copy-start.2 = (f32[12,32,1024]{2,1,0:T(8,128)}, f32[12,32,1024]{2,1,0:T(8,128)S(1)}, u32[]{:S(2)}) copy-start(f32[12,32,1024]{2,1,0:T(8,128)S(1)} %get-tuple-element.6) | copy-start | bytes 4718596
  55.6 468.1 %all-gather.2.cloned.1.call-start = ((), (), s32[]{:S(2)}) async-start(), calls=%async_computation.1 | async-start | bytes 7864320 | tf_op jit(solution)/shard_map/all_gather | solution.py:12
  529.5 9.4 %copy-start.1 = (bf16[1024,32]{0,1:T(8,128)(2,1)S(1)}, bf16[1024,32]{0,1:T(8,128)(2,1)}, u32[]{:S(2)}) copy-start(bf16[1024,32]{0,1:T(8,128)(2,1)} %param.5) | copy-start | bytes 196612
Sparse Core Ops, SparseCore 0:
  55.7 86.5 all-reduce.2
Sparse Core Ops, SparseCore 1:
  57.6 43.5 all-gather.1
where the time goes:
time: 547 us; the launch traced here: 546 us
  blocking collectives  383 us (70%)
  waiting for transfers between devices  66.6 us (12%)
  matrix products  50.8 us (9%)
  local copies, waits for them, and re-layouts  22.2 us (4%)
  between operations  14.9 us (3%)
  other arithmetic  9.19 us (2%)
    psum x1, blocking collectives, shards(): summed = lax.psum(partial_out, 'tok').astype(jnp.bfloat16)  327 us
    psum x1, waiting for transfers between devices, shards(): slot_sum, slot_den = lax.psum((local_sum, local_den), 'tok')  66 us
    pmax x1, blocking collectives, shards(): slot_peak = lax.pmax(local_max, 'tok')  23.4 us
    psum x1, blocking collectives, shards(): slot_sum, slot_den = lax.psum((local_sum, local_den), 'tok')  18.4 us
    all_to_all x1, blocking collectives, shards(): lax.all_to_all(summed, 'exp', split_axis=2, concat_axis=1, tiled=True)  14.2 us
    dot_general x1, matrix products, shards(): jnp.einsum('std,dj->sjt', tokens, slot_params, preferred_element_type=jnp...  12.3 us
    dot_general x1, matrix products, shards(): jnp.einsum('sjt,std->sjd', dweight, tokens, preferred_element_type=jnp.fl...  11.7 us
  transfers between devices with their start and end apart: 2, of which 1 were waited for; matrix products, arithmetic and copies ran while one was open for 8% of the time, Pallas kernels for 0%

commit v1 on v0

--- a/solution.py
+++ b/solution.py
@@ -29,7 +29,10 @@
     partial_out = jnp.einsum("sepf,efd->sepd", hidden, w_out, preferred_element_type=jnp.float32)
     partial_out = partial_out.reshape(seq_count, own_width, width)
     summed = lax.psum(partial_out, "tok").astype(jnp.bfloat16)
-    slot_out = lax.all_to_all(summed, "exp", split_axis=2, concat_axis=1, tiled=True)
+    slot_out = jnp.concatenate(
+        lax.all_to_all(jnp.stack(jnp.split(summed, lax.axis_size("exp"), axis=2)), "exp", 0, 0),
+        axis=1,
+    )
     comb_max = jnp.max(all_logits, axis=1)
     cexp = jnp.exp(all_logits - comb_max[:, None, :])
     cweight = (cexp / jnp.sum(cexp, axis=1)[:, None, :]).astype(jnp.bfloat16)

time: 547 us -> 282 us (0.52)
  blocking collectives: 383 us -> 137 us
  local copies, waits for them, and re-layouts: 22.2 us -> 2.36 us
    psum x1, blocking collectives: 327 us -> 81.3 us  [shards(): summed = lax.psum(partial_out, 'tok').astype(jnp.bfloat16)]
    unnamed x8 -> x6, local copies, waits for them, and re-layouts: 9.98 us -> 0.85 us
    reshape x1, local copies, waits for them, and re-layouts: 6.51 us -> 0.92 us  [shards(): partial_out = partial_out.reshape(seq_count, own_width, width)]
where the time goes in v1:
time: 282 us; the launch traced here: 281 us
  blocking collectives  137 us (49%)
  waiting for transfers between devices  66.7 us (24%)
  matrix products  50.9 us (18%)
  between operations  14.9 us (5%)
  other arithmetic  9.29 us (3%)
    psum x1, blocking collectives, shards(): summed = lax.psum(partial_out, 'tok').astype(jnp.bfloat16)  81.3 us
    psum x1, waiting for transfers between devices, shards(): slot_sum, slot_den = lax.psum((local_sum, local_den), 'tok')  66.2 us
    pmax x1, blocking collectives, shards(): slot_peak = lax.pmax(local_max, 'tok')  23.4 us
    psum x1, blocking collectives, shards(): slot_sum, slot_den = lax.psum((local_sum, local_den), 'tok')  18.4 us
    all_to_all x1, blocking collectives, shards(): lax.all_to_all(jnp.stack(jnp.split(summed, lax.axis_size('exp'), axis=2))...  14.1 us
    dot_general x1, matrix products, shards(): jnp.einsum('std,dj->sjt', tokens, slot_params, preferred_element_type=jnp...  12.3 us
    dot_general x1, matrix products, shards(): jnp.einsum('sjt,std->sjd', dweight, tokens, preferred_element_type=jnp.fl...  11.7 us
    dot_general x1, matrix products, shards(): jnp.einsum('sjt,sjd->std', cweight, slot_out, preferred_element_type=jnp....  9.41 us
  transfers between devices with their start and end apart: 2, of which 1 were waited for; matrix products, arithmetic and copies ran while one was open for 8% of the time, Pallas kernels for 0%

profile of v1, /device:TPU:0, one launch (start us, length us, event | category | flops | bytes accessed | tf_op | source)
XLA Modules:
  0.0 281.3 jit_solution(13637341516667016020)
XLA Ops:
  7.4 0.0 copy-start
  7.4 0.0 all-reduce.3.cloned.1.call-start
  7.4 0.8 copy-done
  8.2 12.3 %fusion.28 = (f32[12,32]{1,0:T(8,128)S(1)}, f32[12,32,1024]{2,1,0:T(8,128)S(1)}) fusion(bf16[12,1024,1024]{2,1,0:T(8,128)(2,1)} %param.4, bf16[1024,32]{0,1:T(8,128)(2,1)S(1)} %copy-done), kind=kOutput, calls=%fused_computation.33 | convolution fusion | flops 805699200 | bytes 26805760 | tf_op jit(solution)/shard_map/std,dj->sjt/dot_general | solution.py:11
  20.5 0.0 copy-start.2
  20.5 23.4 %pmax.7 = f32[12,32]{1,0:T(8,128)S(1)} all-reduce(f32[12,32]{1,0:T(8,128)S(1)} %get-tuple-element.9), channel_id=1, replica_groups=mesh['tok'=8,'exp'=4] {'tok'}, use_global_device_ids=true, to_apply=%region_3.0 | all-reduce | flops 384 | bytes 3072 | tf_op jit(solution)/shard_map/pmax | solution.py:14
  43.9 11.7 %fusion.23 = f32[12,32,1024]{2,1,0:T(8,128)} fusion(bf16[12,1024,1024]{2,1,0:T(8,128)(2,1)} %param.4, f32[12,32,1024]{2,1,0:T(8,128)S(1)} %get-tuple-element.10, f32[12,32]{1,0:T(8,128)S(1)} %pmax.7), kind=kOutput, calls=%fused_computation.24 | convolution fusion | flops 806092800 | bytes 28313088 | tf_op jit(solution)/shard_map/sjt,std->sjd/dot_general | solution.py:18
  55.6 0.0 copy-done.2
  55.6 0.0 all-reduce.3.cloned.1.call-update
  55.6 0.0 all-gather.2.cloned.1.call-start
  55.6 0.5 all-gather.2.cloned.1.call-update
  56.2 1.8 fusion.6
  57.9 18.4 %psum.22 = f32[12,32]{1,0:T(8,128)S(1)} all-reduce(f32[12,32]{1,0:T(8,128)S(1)} %fusion.6), channel_id=1, replica_groups=mesh['tok'=8,'exp'=4] {'tok'}, use_global_device_ids=true, to_apply=%region_6.0 | all-reduce | flops 384 | bytes 3072 | tf_op jit(solution)/shard_map/psum | solution.py:19
  76.3 66.2 %all-reduce.3.cloned.1.call-done = f32[12,32,1024]{2,1,0:T(8,128)} async-done(((f32[12,32,1024]{2,1,0:T(8,128)}), f32[12,32,1024]{2,1,0:T(8,128)}) %all-reduce.3.cloned.1.call-update) | async-done | bytes 1572880 | tf_op jit(solution)/shard_map/psum | solution.py:19
  142.5 1.6 divide_convert_fusion.2
  144.1 0.4 copy.15
  144.6 8.7 %fusion.20 = bf16[12,16,2,512]{3,0,2,1:T(8,128)(2,1)S(1)} fusion(bf16[12,16,2,1024]{3,0,2,1:T(8,128)(2,1)S(1)} %bitcast.51, bf16[16,1024,512]{2,1,0:T(8,128)(2,1)} %param.6), kind=kOutput, calls=%fused_computation.23 | convolution fusion | flops 404422656 | bytes 17956864 | tf_op jit(solution)/shard_map/sepd,edf->sepf/dot_general | solution.py:26
  153.3 8.7 %fusion.1 = f32[16,12,2,1024]{3,1,2,0:T(8,128)S(1)} fusion(bf16[12,16,2,512]{3,0,2,1:T(8,128)(2,1)S(1)} %fusion.20, bf16[16,512,1024]{2,1,0:T(8,128)(2,1)} %param.7), kind=kOutput, calls=%fused_computation.1 | convolution fusion | flops 402653184 | bytes 18743296 | tf_op jit(solution)/shard_map/sepf,efd->sepd/dot_general | solution.py:29
  162.0 0.9 copy.9
  163.0 81.3 %all-reduce.4 = bf16[12,32,1024]{2,1,0:T(8,128)(2,1)S(1)} all-reduce(f32[12,32,1024]{2,1,0:T(8,128)S(1)} %copy.9), channel_id=1, replica_groups=mesh['tok'=8,'exp'=4] {'tok'}, use_global_device_ids=true, to_apply=%region_7.0 | all-reduce | flops 393216 | bytes 2359296 | tf_op jit(solution)/shard_map/psum | solution.py:31
  244.3 0.1 slice_bitcast_fusion.3
  244.4 0.1 pad_maximum_fusion
  244.5 14.1 %all_to_all.5 = bf16[4,12,32,256]{3,2,1,0:T(8,128)(2,1)S(1)} all-to-all(bf16[4,12,32,256]{3,2,1,0:T(8,128)(2,1)S(1)} %pad_maximum_fusion), channel_id=1, replica_groups=mesh['tok'=8,'exp'=4] {'exp'}, dimensions={0} | all-to-all | bytes 1572864 | tf_op jit(solution)/shard_map/all_to_all | solution.py:33
  258.6 0.1 copy.10
  258.6 0.0 all-gather.2.cloned.1.call-done
  258.7 5.8 %fusion.29 = f32[12,1024]{1,0:T(8,128)S(1)} fusion(f32[12,128,1024]{2,1,0:T(8,128)} %all-gather.2.cloned.1.call-done), kind=kOutput, calls=%fused_computation.34 | output fusion | flops 3145855 | bytes 6340608 | tf_op jit(solution)/shard_map/sub | solution.py:37
  264.5 0.0 copy-start.1
  264.5 9.4 %convolution_convert_fusion = bf16[12,1024,256]{2,1,0:T(8,128)(2,1)} fusion(bf16[12,128,256]{2,1,0:T(8,128)(2,1)S(1)} %bitcast.53, f32[12,1024]{1,0:T(8,128)S(1)} %fusion.29, f32[12,128,1024]{2,1,0:T(8,128)} %all-gather.2.cloned.1.call-done), kind=kOutput, calls=%fused_computation.7 | convolution fusion | flops 813183104 | bytes 13418496 | tf_op jit(solution)/shard_map/sjt,sjd->std/dot_general | solution.py:39
  273.9 0.0 copy-done.1
Async XLA Ops:
  7.4 0.8 copy-start
  7.4 135.1 %all-reduce.3.cloned.1.call-start = ((), (), s32[]{:S(2)}) async-start(), calls=%async_computation.2 | async-start | bytes 3145728 | tf_op jit(solution)/shard_map/psum | solution.py:19
  20.5 35.0 %copy-start.2 = (f32[12,32,1024]{2,1,0:T(8,128)}, f32[12,32,1024]{2,1,0:T(8,128)S(1)}, u32[]{:S(2)}) copy-start(f32[12,32,1024]{2,1,0:T(8,128)S(1)} %get-tuple-element.10) | copy-start | bytes 4718596
  55.6 203.1 %all-gather.2.cloned.1.call-start = ((), (), s32[]{:S(2)}) async-start(), calls=%async_computation.1 | async-start | bytes 7864320 | tf_op jit(solution)/shard_map/all_gather | solution.py:12
  264.5 9.4 %copy-start.1 = (bf16[1024,32]{0,1:T(8,128)(2,1)S(1)}, bf16[1024,32]{0,1:T(8,128)(2,1)}, u32[]{:S(2)}) copy-start(bf16[1024,32]{0,1:T(8,128)(2,1)} %param.5) | copy-start | bytes 196612
Sparse Core Ops, SparseCore 0:
  55.7 86.7 all-reduce.2
Sparse Core Ops, SparseCore 1:
  57.6 43.5 all-gather.1
